TPU v7x, 32 devices: a whole 2x2x4 slice. The times are simulated.
32 devices in a mesh: grp: 8 (over z, x), tp: 4 (over y, core).
Axes of the slice: x: 2, y: 2, z: 4, core: 2. Of those that a mesh axis runs over, the one named last changes fastest.
Arguments:
- suffix_cache: bfloat16 [32, 512, 2, 1024], P('grp', None, None, 'tp'), may hold values from -6 to 6
- prompt_cache: bfloat16 [16, 512, 2, 1024], P('grp', None, None, 'tp'), may hold values from -6 to 6
- query_first: bfloat16 [32, 8192], P('grp', 'tp'), may hold values from -45 to 45
- fresh_first: bfloat16 [32, 2, 1024], P('grp', None, 'tp'), may hold values from -6 to 6
- query_second: bfloat16 [32, 8192], P('grp', 'tp'), may hold values from -45 to 45
- fresh_second: bfloat16 [32, 2, 1024], P('grp', None, 'tp'), may hold values from -6 to 6
- out_weight: bfloat16 [8192, 4096], P('tp'), may hold values from -1 to 1
- suffix_len: int32 [32], replicated, may hold values from 0 to 511, as said below
- prompt_slot: int32 [32], P('grp'), may hold values from -1 to 1, as said below
- moves: int32 [2, 5], replicated, may hold values from 0 to 7, as said below
Outputs:
- out_first: bfloat16 [32, 4096], P('grp', 'tp')
- out_second: bfloat16 [32, 4096], P('grp', 'tp')
Inputs may be any that keep to these rules, and one draw needn't show every extreme that they name: `suffix_len`: 0 exactly on empty slots, 1 or more on live ones. Every group has exactly one empty slot before the migration. The source of every move is live and its length is 384 or more; some source has 511. `prompt_slot`: each group's live samples read its prompt slots; in every destination group all live samples read one prompt slot and the other is free. `moves`: source groups are distinct, destination groups are distinct, and no group is both. The destination slot is the destination group's empty slot and the destination prompt slot is its free prompt slot.
All inputs are finite; a program needn't handle non-finite values.
Results may differ from a plain program's by a relative error of at most 0.0058.
Values may be sent and summed in bfloat16 or wider, within the bound.
A program may use at most 128 MiB of HBM per device.

v0:
```python
import jax
import jax.numpy as jnp
from jax import lax
from jax.sharding import PartitionSpec as P

QH = 64
KVH = 8
HD = 128


def attend_slots(queries, prompt_kv, suffix_kv, fresh, lengths, prompt_ids):
    samples = queries.shape[0]
    kv_heads = suffix_kv.shape[3] // HD
    share = QH // KVH
    prompt_len = prompt_kv.shape[1]
    suffix_cap = suffix_kv.shape[1]
    chooser = (prompt_ids[:, None] == jnp.arange(prompt_kv.shape[0])[None, :]).astype(jnp.bfloat16)
    chosen = jnp.einsum(
        "sp,pltw->sltw", chooser, prompt_kv, preferred_element_type=jnp.float32
    ).astype(jnp.bfloat16)
    key_rows = jnp.concatenate([chosen[:, :, 0], suffix_kv[:, :, 0]], 1).reshape(
        samples, -1, kv_heads, HD
    )
    value_rows = jnp.concatenate([chosen[:, :, 1], suffix_kv[:, :, 1]], 1).reshape(
        samples, -1, kv_heads, HD
    )
    heads = queries.reshape(samples, kv_heads, share, HD)
    scale = HD ** (-0.5)
    scores = (
        jnp.einsum("skgd,slkd->skgl", heads, key_rows, preferred_element_type=jnp.float32) * scale
    )
    fresh_keys = fresh[:, 0].reshape(samples, kv_heads, HD)
    own_score = (
        jnp.einsum("skgd,skd->skg", heads, fresh_keys, preferred_element_type=jnp.float32) * scale
    )
    valid = jnp.concatenate(
        [jnp.ones((samples, prompt_len), bool), jnp.arange(suffix_cap)[None, :] < lengths[:, None]],
        1,
    )
    scores = jnp.where(valid[:, None, None, :], scores, -1e30)
    highest = jnp.maximum(jnp.max(scores, -1), own_score)
    spread = jnp.exp(scores - highest[..., None])
    own_spread = jnp.exp(own_score - highest)
    total = jnp.sum(spread, -1) + own_spread
    weights = (spread / total[..., None]).astype(jnp.bfloat16)
    own_weight = (own_spread / total).astype(jnp.bfloat16)
    mixed = jnp.einsum("skgl,slkd->skgd", weights, value_rows, preferred_element_type=jnp.float32)
    fresh_values = fresh[:, 1].reshape(samples, kv_heads, 1, HD).astype(jnp.float32)
    mixed = mixed + own_weight.astype(jnp.float32)[..., None] * fresh_values
    live = prompt_ids >= 0
    return jnp.where(live[:, None], mixed.reshape(samples, -1), 0.0).astype(jnp.bfloat16)


def pick_field(hit, move_rows, column):
    return jnp.sum(jnp.where(hit, move_rows[:, column], 0))


def per_device(
    suffix_cache,
    prompt_cache,
    query_first,
    fresh_first,
    query_second,
    fresh_second,
    out_weight,
    suffix_len,
    prompt_slot,
    moves,
):
    slot_count = suffix_cache.shape[0]
    suffix_cap = suffix_cache.shape[1]
    own_group = lax.axis_index("grp")
    row_base = own_group * slot_count
    lengths = lax.dynamic_slice_in_dim(suffix_len, row_base, slot_count)
    attn_first = attend_slots(
        query_first, prompt_cache, suffix_cache, fresh_first, lengths, prompt_slot
    )
    positions = jnp.arange(suffix_cap)
    write_mask = (positions[None, :] == lengths[:, None]) & (prompt_slot[:, None] >= 0)
    appended = jnp.where(write_mask[:, :, None, None], fresh_first[:, None], suffix_cache)
    source_hit = moves[:, 0] == own_group
    target_hit = moves[:, 2] == own_group
    is_source = jnp.any(source_hit)
    is_target = jnp.any(target_hit)
    out_slot = pick_field(source_hit, moves, 1)
    destination = pick_field(source_hit, moves, 2)
    in_source = pick_field(target_hit, moves, 0)
    in_from_slot = pick_field(target_hit, moves, 1)
    in_slot = pick_field(target_hit, moves, 3)
    in_prompt = pick_field(target_hit, moves, 4)
    sample_rows = lax.dynamic_index_in_dim(appended, out_slot, 0, keepdims=False)
    prompt_index = jnp.maximum(
        lax.dynamic_index_in_dim(prompt_slot, out_slot, 0, keepdims=False), 0
    )
    prompt_rows = lax.dynamic_index_in_dim(prompt_cache, prompt_index, 0, keepdims=False)
    packed = jnp.concatenate([sample_rows, prompt_rows], 0)
    peer_count = lax.axis_size("grp")
    lane_mask = (jnp.arange(peer_count) == destination) & is_source
    outgoing = jnp.where(lane_mask[:, None, None, None], packed[None], jnp.zeros((), jnp.bfloat16))
    received = lax.all_to_all(outgoing, "grp", split_axis=0, concat_axis=0, tiled=True)
    arrived = lax.dynamic_index_in_dim(received, in_source, 0, keepdims=False)
    suffix_in = arrived[:suffix_cap]
    prompt_in = arrived[suffix_cap:]
    slot_ids = jnp.arange(slot_count)
    into_slot = (slot_ids == in_slot) & is_target
    leaving = (slot_ids == out_slot) & is_source
    suffix_moved = jnp.where(into_slot[:, None, None, None], suffix_in[None], appended)
    into_prompt = (jnp.arange(prompt_cache.shape[0]) == in_prompt) & is_target
    prompt_moved = jnp.where(into_prompt[:, None, None, None], prompt_in[None], prompt_cache)
    in_length = (
        lax.dynamic_index_in_dim(
            suffix_len, in_source * slot_count + in_from_slot, 0, keepdims=False
        )
        + 1
    )
    grown = jnp.where(prompt_slot >= 0, lengths + 1, 0)
    length_moved = jnp.where(into_slot, in_length, jnp.where(leaving, 0, grown))
    slot_moved = jnp.where(into_slot, in_prompt, jnp.where(leaving, -1, prompt_slot))
    attn_second = attend_slots(
        query_second, prompt_moved, suffix_moved, fresh_second, length_moved, slot_moved
    )
    proj_first = jnp.dot(attn_first, out_weight, preferred_element_type=jnp.float32)
    proj_second = jnp.dot(attn_second, out_weight, preferred_element_type=jnp.float32)
    out_first, out_second = (
        lax.psum_scatter(proj_first, "tp", scatter_dimension=1, tiled=True),
        lax.psum_scatter(proj_second, "tp", scatter_dimension=1, tiled=True),
    )
    return (out_first.astype(jnp.bfloat16), out_second.astype(jnp.bfloat16))


def solution(mesh):
    placed = (
        P("grp", None, None, "tp"),
        P("grp", None, None, "tp"),
        P("grp", "tp"),
        P("grp", None, "tp"),
        P("grp", "tp"),
        P("grp", None, "tp"),
        P("tp", None),
        P(),
        P("grp"),
        P(),
    )
    return jax.shard_map(
        per_device,
        mesh=mesh,
        in_specs=placed,
        out_specs=(P("grp", "tp"), P("grp", "tp")),
        check_vma=False,
    )
```

profile of v0, /device:TPU:0, one launch (start us, length us, event | category | flops | bytes accessed | tf_op | source)
XLA Modules:
  0.0 297.1 jit_solution(12544369144469086026)
XLA Ops:
  12.4 4.7 %copy.56 = bf16[4,512,2,256]{1,3,0,2:T(8,128)(2,1)S(1)} copy(bf16[4,512,2,256]{3,2,1,0:T(2,128)(2,1)} %param.10) | data formatting | bytes 4194304 | tf_op args[0]
  20.3 3.2 %broadcast_compare_fusion.2 = (pred[4]{0:T(512)(128)(4,1)S(1)}, s32[4]{0:T(128)S(1)}, pred[4]{0:T(512)(128)(4,1)S(1)}, pred[4]{0:T(512)(128)(4,1)S(1)}) fusion(s32[4]{0:T(128)S(1)} %copy-done.11, pred[]{:T(512)} %fusion.93, s32[]{:T(128)} %get-tuple-element.8, s32[]{:T(128)} %get-tuple-element.11, pred[]{:T(512)} %reduce_or.18, s32[]{:T(128)} %get-tuple-element.12), kind=kLoop, calls=%fused_computation.115 | loop fusion | flops 32 | bytes 58 | tf_op jit(solution)/shard_map/ge | solution.py:50
  26.2 2.0 copy.65
  30.4 1.5 copy.67
  33.3 3.8 %broadcast_select_fusion = bf16[8,1024,2,256]{1,3,2,0:T(8,128)(2,1)} fusion(pred[8]{0:T(512)(128)(4,1)S(1)} %compare_and_fusion, bf16[1024,2,256]{0,2,1:T(8,128)(2,1)S(1)} %copy.67), kind=kLoop, calls=%fused_computation | loop fusion | flops 4194304 | bytes 9437192 | tf_op jit(solution)/shard_map/jit(_where)/select_n | solution.py:99
  37.1 7.3 %all-to-all-start = ((bf16[8,1024,2,256]{1,3,2,0:T(8,128)(2,1)}), bf16[8,1024,2,256]{1,3,2,0:T(8,128)(2,1)}, u32[]{:S(2)}, u32[]{:S(2)}) async-start(bf16[8,1024,2,256]{1,3,2,0:T(8,128)(2,1)} %broadcast_select_fusion), calls=%async_computation | async-start | bytes 16777216 | tf_op jit(solution)/shard_map/all_to_all | solution.py:100
  47.0 3.1 %convolution_convert_fusion.1 = bf16[4,512,2,256]{3,0,2,1:T(4,128)(2,1)S(1)} fusion(bf16[2,512,2,256]{3,2,1,0:T(2,128)(2,1)} %param.11, s32[4]{0:T(128)S(1)} %copy-done.11), kind=kOutput, calls=%fused_computation.23 | convolution fusion | flops 5242888 | bytes 3145744 | tf_op jit(solution)/shard_map/sp,pltw->sltw/dot_general | solution.py:18
  50.1 2.0 fusion.96
  52.1 1.5 concatenate.42
  54.7 2.3 copy.62
  57.0 1.5 concatenate.45
  61.7 11.6 %convolution_bitcast_fusion.1 = f32[4096,4]{1,0:T(8,128)} fusion(bf16[2048,4096]{1,0:T(8,128)(2,1)} %param.16, bf16[1,4,16,128]{3,2,1,0:T(8,128)(2,1)S(1)} %fusion.43, pred[4]{0:T(512)(128)(4,1)S(1)} %get-tuple-element.39), kind=kOutput, calls=%fused_computation.2 | convolution fusion | flops 67117056 | bytes 16859140
  77.0 150.5 %all-to-all-done = bf16[8,1024,2,256]{1,3,2,0:T(8,128)(2,1)} async-done(((bf16[8,1024,2,256]{1,3,2,0:T(8,128)(2,1)}), bf16[8,1024,2,256]{1,3,2,0:T(8,128)(2,1)}, u32[]{:S(2)}, u32[]{:S(2)}) %all-to-all-start) | async-done | bytes 8388640 | tf_op jit(solution)/shard_map/all_to_all | solution.py:100
  227.5 2.3 dynamic-slice_bitcast_fusion.1
  229.9 2.0 copy.68
  231.9 2.2 broadcast_select_fusion.1
  234.1 1.8 convolution_convert_fusion
  235.8 2.1 fusion.94
  237.9 1.5 concatenate.50
  242.4 2.0 fusion.99
  246.4 11.6 %convolution_bitcast_fusion = f32[4096,4]{1,0:T(8,128)} fusion(bf16[2048,4096]{1,0:T(8,128)(2,1)} %param.16, bf16[1,4,16,128]{3,2,1,0:T(8,128)(2,1)S(1)} %fusion.37, pred[4]{0:T(512)(128)(4,1)S(1)} %get-tuple-element.13), kind=kOutput, calls=%fused_computation.1 | convolution fusion | flops 67117056 | bytes 16859140
  258.0 1.8 copy.82
  259.9 28.5 %reduce-scatter.9.cloned.1.call-done = f32[1024,4]{1,0:T(8,128)} async-done(((f32[4096,4]{1,0:T(8,128)}), f32[1024,4]{1,0:T(8,128)}) %reduce-scatter.9.cloned.1.call-update) | async-done | bytes 16400
  288.4 1.8 copy.84
  (79 shorter events, 23.4 us)
Async XLA Ops:
  12.3 4.8 %copy-start.9 = (bf16[4,2,256]{2,1,0:T(2,128)(2,1)S(1)}, bf16[4,2,256]{2,1,0:T(2,128)(2,1)}, u32[]{:S(2)}) copy-start(bf16[4,2,256]{2,1,0:T(2,128)(2,1)} %param.13) | copy-start | bytes 12292
  12.4 4.8 %copy-start.12 = (s32[32]{0:T(128)S(1)}, s32[32]{0:T(128)}, u32[]{:S(2)}) copy-start(s32[32]{0:T(128)} %param.17) | copy-start | bytes 388
  12.4 7.4 %copy-start.11 = (s32[4]{0:T(128)S(1)}, s32[4]{0:T(128)}, u32[]{:S(2)}) copy-start(s32[4]{0:T(128)} %param.18) | copy-start | bytes 52
  25.4 3.5 %copy-start.1 = (bf16[2,512,2,256]{3,2,1,0:T(2,128)(2,1)S(1)}, bf16[2,512,2,256]{3,2,1,0:T(2,128)(2,1)}, u32[]{:S(2)}) copy-start(bf16[2,512,2,256]{3,2,1,0:T(2,128)(2,1)} %param.11) | copy-start | bytes 3145732
  28.3 1.1 copy-start.3
  37.1 190.4 %all-to-all-start = ((bf16[8,1024,2,256]{1,3,2,0:T(8,128)(2,1)}), bf16[8,1024,2,256]{1,3,2,0:T(8,128)(2,1)}, u32[]{:S(2)}, u32[]{:S(2)}) async-start(bf16[8,1024,2,256]{1,3,2,0:T(8,128)(2,1)} %broadcast_select_fusion), calls=%async_computation | async-start | bytes 16777216 | tf_op jit(solution)/shard_map/all_to_all | solution.py:100
  44.4 213.7 %reduce-scatter.7.cloned.1.call-start = ((), (), s32[]{:S(2)}) async-start(), calls=%async_computation.3 | async-start | bytes 2621440
  57.0 1.7 copy-start.13
  58.5 1.2 copy-start.5
  58.5 1.5 copy-start.7
  60.1 1.2 copy-start.6
  73.3 1.6 copy-start.10
  73.3 3.6 %copy-start.14 = (bf16[4,2048]{1,0:T(4,128)(2,1)S(1)}, bf16[4,2048]{1,0:T(4,128)(2,1)}, u32[]{:S(2)}) copy-start(bf16[4,2048]{1,0:T(4,128)(2,1)} %param.14) | copy-start | bytes 49156
  73.3 158.6 %copy-start.2 = (bf16[2,512,2,256]{3,2,1,0:T(2,128)(2,1)S(1)}, bf16[2,512,2,256]{3,2,1,0:T(2,128)(2,1)}, u32[]{:S(2)}) copy-start(bf16[2,512,2,256]{3,2,1,0:T(2,128)(2,1)} %param.11) | copy-start | bytes 3145732
  73.3 215.1 %reduce-scatter.9.cloned.1.call-start = ((), (), s32[]{:S(2)}) async-start(), calls=%async_computation.4 | async-start | bytes 2621440
  239.4 1.2 copy-start.4
  241.1 1.3 copy-start.8
  242.4 2.3 copy-start
Sparse Core Ops, SparseCore 0:
  73.4 32.5 reduce-scatter.6
  258.1 30.2 reduce-scatter.8
where the time goes:
time: 298 us; the launch traced here: 297 us
  waiting for transfers between devices  179 us (60%)
  local copies, waits for them, and re-layouts  39.9 us (13%)
  matrix products  31.9 us (11%)
  between operations  21.1 us (7%)
  other arithmetic  17.6 us (6%)
  starting transfers between devices  7.54 us (3%)
    all_to_all x1, waiting for transfers between devices, per_device(): lax.all_to_all(outgoing, 'grp', split_axis=0, concat_axis=0, tiled=True)  151 us
    unnamed x4, waiting for transfers between devices  28.6 us
    unnamed x2, matrix products  23.1 us
    unnamed x35, local copies, waits for them, and re-layouts  10 us
    concatenate x6, local copies, waits for them, and re-layouts, attend_slots(): jnp.concatenate([chosen[:, :, 0], suffix_kv[:, :, 0]], 1)  7.85 us
    all_to_all x1, starting transfers between devices, per_device(): lax.all_to_all(outgoing, 'grp', split_axis=0, concat_axis=0, tiled=True)  7.28 us
  transfers between devices with their start and end apart: 3, of which 2 were waited for; matrix products, arithmetic and copies ran while one was open for 21% of the time, Pallas kernels for 0%

commit v1 on v0

v1 whole, which is shorter than its diff:
```python
import functools

import jax
import jax.numpy as jnp
from jax import lax
from jax.experimental import pallas as pl
from jax.experimental.pallas import tpu as pltpu
from jax.sharding import PartitionSpec as P

QH = 64
KVH = 8
HD = 128
MESH = pl.DeviceIdType.MESH
F32 = jnp.float32
BF16 = jnp.bfloat16


def kernel(
    groups,
    ranks,
    lens_ref,
    pslot_ref,
    moves_ref,
    suffix_hbm,
    prompt_hbm,
    q1_ref,
    f1_ref,
    q2_ref,
    f2_ref,
    weight_hbm,
    out_ref,
    sbuf,
    pbuf,
    wbuf,
    qs,
    fs,
    packets,
    parts_out,
    parts_in,
    rows_back,
    kv_sem,
    w_sem,
    g_send,
    g_recv,
    r_send,
    r_recv,
    b_send,
    b_recv,
):
    me = lax.axis_index("grp")
    rank = lax.axis_index("tp")
    slots = q1_ref.shape[0]
    prompts = prompt_hbm.shape[0]
    features = q1_ref.shape[1]
    heads = features // HD
    share = QH // KVH
    kv_heads = heads // share
    width = kv_heads * HD
    cap = suffix_hbm.shape[1]
    plen = prompt_hbm.shape[1]
    cols = out_ref.shape[1]
    move_count = moves_ref.shape[0]

    def kv_copies():
        copies = []
        for k in range(kv_heads):
            lanes = pl.ds(k * HD, HD)
            for p in range(prompts):
                copies.append(
                    pltpu.make_async_copy(
                        prompt_hbm.at[p, :, :, lanes], pbuf.at[p, k], kv_sem.at[p, k]
                    )
                )
            for s in range(slots):
                copies.append(
                    pltpu.make_async_copy(
                        suffix_hbm.at[s, :, :, lanes], sbuf.at[s, k], kv_sem.at[prompts + s, k]
                    )
                )
        return copies

    def weight_copy(t):
        j = lax.rem(rank + t, ranks)
        return pltpu.make_async_copy(
            weight_hbm.at[:, pl.ds(pl.multiple_of(j * cols, cols), cols)], wbuf.at[t], w_sem.at[t]
        )

    barrier = pltpu.get_barrier_semaphore()
    for t in range(1, groups):
        pl.semaphore_signal(
            barrier, inc=1, device_id=(lax.rem(me + t, groups), rank), device_id_type=MESH
        )
    for t in range(1, ranks):
        pl.semaphore_signal(
            barrier, inc=1, device_id=(me, lax.rem(rank + t, ranks)), device_id_type=MESH
        )

    for copy in kv_copies():
        copy.start()
    steps = [t % ranks for t in range(1, ranks + 1)]
    for t in steps:
        weight_copy(t).start()

    zero = jnp.int32(0)
    out_slot, into_group, in_slot, from_group = zero - 1, zero, zero - 1, zero
    for m in range(move_count):
        leaves = moves_ref[m, 0] == me
        enters = moves_ref[m, 2] == me
        out_slot = jnp.where(leaves, moves_ref[m, 1], out_slot)
        into_group = jnp.where(leaves, moves_ref[m, 2], into_group)
        in_slot = jnp.where(enters, moves_ref[m, 3], in_slot)
        from_group = jnp.where(enters, moves_ref[m, 0], from_group)

    q2 = q2_ref[...].astype(F32)
    row_ids = lax.broadcasted_iota(jnp.int32, (slots, 1), 0)
    own_row = jnp.sum(jnp.where(row_ids == in_slot, q2, 0.0), 0, keepdims=True)
    fresh2 = [f2_ref[s].astype(F32) for s in range(slots)]
    own_fresh = jnp.zeros((2, width), F32)
    for s in range(slots):
        own_fresh = jnp.where(in_slot == s, fresh2[s], own_fresh)
    packets[me, :, :features] = own_row
    packets[me, :, features : features + width] = own_fresh[0:1]
    packets[me, :, features + width :] = own_fresh[1:2]

    pl.semaphore_wait(barrier, groups - 1 + ranks - 1)

    def gather_copy(t):
        return pltpu.make_async_remote_copy(
            src_ref=packets.at[me],
            dst_ref=packets.at[me],
            send_sem=g_send.at[t],
            recv_sem=g_recv.at[t],
            device_id=(lax.rem(me + t, groups), rank),
            device_id_type=MESH,
        )

    for t in range(1, groups):
        gather_copy(t).start()

    qs[0:slots] = q1_ref[...].astype(F32)
    for s in range(slots):
        fs[s, 0:2] = f1_ref[s].astype(F32)

    for t in range(1, groups):
        gather_copy(t).wait()

    foreign = packets[into_group]
    qs[slots : 2 * slots] = jnp.where(row_ids == out_slot, foreign[:, :features], q2)
    foreign_fresh = jnp.concatenate(
        [foreign[:, features : features + width], foreign[:, features + width :]], 0
    )
    for s in range(slots):
        fs[s, 2:4] = jnp.where(out_slot == s, foreign_fresh, fresh2[s])
        fs[s, 4:8] = jnp.zeros((4, width), F32)

    rows = 2 * slots
    total = heads * rows
    mine = 2 * heads
    stacked = jnp.concatenate([qs[:, j * HD : (j + 1) * HD] for j in range(heads)], 0).astype(BF16)
    def source_of(r):
        s = r // mine
        k = (r % mine) // (2 * share)
        step = (r % (2 * share)) // share
        g = r % share
        return (k * share + g) * rows + step * slots + s

    swap = (
        source_of(lax.broadcasted_iota(jnp.int32, (total, total), 0))
        == lax.broadcasted_iota(jnp.int32, (total, total), 1)
    ).astype(F32).astype(BF16)
    back = (
        source_of(lax.broadcasted_iota(jnp.int32, (total, total), 1))
        == lax.broadcasted_iota(jnp.int32, (total, total), 0)
    ).astype(F32).astype(BF16)
    queries = jnp.dot(swap, stacked, preferred_element_type=F32)

    for copy in kv_copies():
        copy.wait()

    scale = HD ** (-0.5)
    nt = (((1,), (1,)), ((), ()))
    q_row = lax.broadcasted_iota(jnp.int32, (mine, 1), 0)
    second = (q_row % (2 * share)) >= share
    p_col = lax.broadcasted_iota(jnp.int32, (1, 2 * plen), 1)
    s_col = lax.broadcasted_iota(jnp.int32, (1, 2 * cap), 1)
    f_col = lax.broadcasted_iota(jnp.int32, (1, 8), 1)
    p_valid = (p_col % 2) == 0
    f_valid = (f_col == 0) | ((f_col == 2) & second)
    low = -1e30
    results = []
    for s in range(slots):
        q = queries[s * mine : (s + 1) * mine]
        wide = jnp.concatenate(
            [
                jnp.where((q_row // (2 * share)) == k, q, 0.0)
                for k in range(kv_heads)
            ],
            1,
        ).astype(BF16)
        chosen = pslot_ref[s]
        live = chosen >= 0
        row = jnp.maximum(chosen, 0)
        n = lens_ref[me * slots + s]
        xp = jnp.concatenate(
            [pbuf.reshape(prompts, kv_heads, 2 * plen, HD)[row, k] for k in range(kv_heads)], 1
        )
        xs = jnp.concatenate(
            [sbuf.reshape(slots, kv_heads, 2 * cap, HD)[s, k] for k in range(kv_heads)], 1
        )
        xf = fs[s].astype(BF16)
        sp = lax.dot_general(wide, xp, nt, preferred_element_type=F32) * scale
        ss = lax.dot_general(wide, xs, nt, preferred_element_type=F32) * scale
        sf = lax.dot_general(wide, xf, nt, preferred_element_type=F32) * scale
        s_valid = ((s_col % 2) == 0) & (s_col < 2 * n)
        sp = jnp.where(p_valid, sp, low)
        ss = jnp.where(s_valid, ss, low)
        sf = jnp.where(f_valid, sf, low)
        top = jnp.maximum(
            jnp.maximum(jnp.max(sp, 1, keepdims=True), jnp.max(ss, 1, keepdims=True)),
            jnp.max(sf, 1, keepdims=True),
        )
        ep, es, ef = jnp.exp(sp - top), jnp.exp(ss - top), jnp.exp(sf - top)
        sum_all = (
            jnp.sum(ep, 1, keepdims=True)
            + jnp.sum(es, 1, keepdims=True)
            + jnp.sum(ef, 1, keepdims=True)
        )
        inv = 1.0 / sum_all

        def shifted(e):
            w = e * inv
            return jnp.concatenate(
                [
                    pltpu.roll(w[:, i : i + HD], 1, 1)
                    for i in range(0, e.shape[1], HD)
                ],
                1,
            ).astype(BF16)

        mixed = jnp.dot(shifted(ep), xp, preferred_element_type=F32)
        mixed += jnp.dot(shifted(es), xs, preferred_element_type=F32)
        wf = (ef * inv).astype(BF16).astype(F32)
        fval = fs[s]
        mixed += wf[:, 0:1] * fval[1:2] + wf[:, 2:3] * fval[3:4]
        picked = mixed[:, :HD]
        for k in range(1, kv_heads):
            picked = jnp.where((q_row // (2 * share)) == k, mixed[:, k * HD : (k + 1) * HD], picked)
        results.append(jnp.where(live, picked, 0.0))
    attn = jnp.concatenate(results, 0).astype(BF16)
    attn = jnp.dot(back, attn, preferred_element_type=F32)
    attn = jnp.concatenate([attn[j * rows : (j + 1) * rows] for j in range(heads)], 1).astype(BF16)

    def part_copy(t):
        return pltpu.make_async_remote_copy(
            src_ref=parts_out.at[t],
            dst_ref=parts_in.at[t],
            send_sem=r_send.at[t],
            recv_sem=r_recv.at[t],
            device_id=(me, lax.rem(rank + t, ranks)),
            device_id_type=MESH,
        )

    result = None
    for t in steps:
        weight_copy(t).wait()
        part = jnp.dot(attn, wbuf[t], preferred_element_type=F32)
        if t:
            parts_out[t] = part.astype(BF16)
            part_copy(t).start()
        else:
            result = part
    for t in range(1, ranks):
        part_copy(t).wait()
        result += parts_in[t].astype(F32)

    out_rows = lax.broadcasted_iota(jnp.int32, (rows, 1), 0)
    going = (out_rows == slots + out_slot) & (out_slot >= 0)
    rows_back[me] = jnp.sum(jnp.where(going, result, 0.0), 0, keepdims=True)

    def back_copy(t):
        return pltpu.make_async_remote_copy(
            src_ref=rows_back.at[me],
            dst_ref=rows_back.at[me],
            send_sem=b_send.at[t],
            recv_sem=b_recv.at[t],
            device_id=(lax.rem(me + t, groups), rank),
            device_id_type=MESH,
        )

    for t in range(1, groups):
        back_copy(t).start()
    for t in range(1, groups):
        back_copy(t).wait()
    coming = (out_rows == slots + in_slot) & (in_slot >= 0)
    result = jnp.where(coming, rows_back[from_group], jnp.where(going, 0.0, result))
    out_ref[...] = result.astype(BF16)


def per_device(
    suffix_cache,
    prompt_cache,
    query_first,
    fresh_first,
    query_second,
    fresh_second,
    out_weight,
    suffix_len,
    prompt_slot,
    moves,
):
    groups, ranks = lax.axis_size("grp"), lax.axis_size("tp")
    slots, features = query_first.shape
    prompts, plen = prompt_cache.shape[:2]
    cap = suffix_cache.shape[1]
    width = suffix_cache.shape[3]
    kv_heads = width // HD
    cols = out_weight.shape[1] // ranks
    depth = out_weight.shape[0]
    vmem = pl.BlockSpec(memory_space=pltpu.VMEM)
    smem = pl.BlockSpec(memory_space=pltpu.SMEM)
    hbm = pl.BlockSpec(memory_space=pltpu.HBM)
    dma = pltpu.SemaphoreType.DMA
    out = pl.pallas_call(
        functools.partial(kernel, groups, ranks),
        out_shape=jax.ShapeDtypeStruct((2 * slots, cols), BF16),
        in_specs=[smem, smem, smem, hbm, hbm, vmem, vmem, vmem, vmem, hbm],
        out_specs=vmem,
        scratch_shapes=[
            pltpu.VMEM((slots, kv_heads, cap, 2, HD), BF16),
            pltpu.VMEM((prompts, kv_heads, plen, 2, HD), BF16),
            pltpu.VMEM((ranks, depth, cols), BF16),
            pltpu.VMEM((2 * slots, features), F32),
            pltpu.VMEM((slots, 8, width), F32),
            pltpu.VMEM((groups, 1, features + 2 * width), F32),
            pltpu.VMEM((ranks, 2 * slots, cols), BF16),
            pltpu.VMEM((ranks, 2 * slots, cols), BF16),
            pltpu.VMEM((groups, 1, cols), F32),
            dma((prompts + slots, kv_heads)),
            dma((ranks,)),
            dma((groups,)),
            dma((groups,)),
            dma((ranks,)),
            dma((ranks,)),
            dma((groups,)),
            dma((groups,)),
        ],
        compiler_params=pltpu.CompilerParams(
            collective_id=0, has_side_effects=True, vmem_limit_bytes=48 * 1024 * 1024
        ),
    )(
        suffix_len,
        prompt_slot,
        moves,
        suffix_cache,
        prompt_cache,
        query_first,
        fresh_first,
        query_second,
        fresh_second,
        out_weight,
    )
    return out[:slots], out[slots:]


def solution(mesh):
    placed = (
        P("grp", None, None, "tp"),
        P("grp", None, None, "tp"),
        P("grp", "tp"),
        P("grp", None, "tp"),
        P("grp", "tp"),
        P("grp", None, "tp"),
        P("tp", None),
        P(),
        P("grp"),
        P(),
    )
    return jax.shard_map(
        per_device,
        mesh=mesh,
        in_specs=placed,
        out_specs=(P("grp", "tp"), P("grp", "tp")),
        check_vma=False,
    )
```

time: 298 us -> 33.8 us (0.11)
  waiting for transfers between devices: 179 us -> 0 us
  matrix products: 31.9 us -> 0 us
  local copies, waits for them, and re-layouts: 39.9 us -> 8.21 us
  Pallas kernels: 0 us -> 24.5 us
  between operations: 21.1 us -> 0.66 us
  other arithmetic: 17.6 us -> 0 us
  starting transfers between devices: 7.54 us -> 0 us
    all_to_all x1 -> x0, waiting for transfers between devices: 151 us -> none  [per_device(): lax.all_to_all(outgoing, 'grp', split_axis=0, concat_axis=0, tiled=True)]
    unnamed x4 -> x0, waiting for transfers between devices: 28.6 us -> none
    pallas_call x0 -> x1, Pallas kernels: none -> 24.5 us  [per_device(): pl.pallas_call(functools.partial(kernel, groups, ranks), out_shape=jax.Sh...]
    unnamed x2 -> x0, matrix products: 23.1 us -> none
    concatenate x15 -> x0, local copies, waits for them, and re-layouts: 14.5 us -> none  [the longest x6 7.85 us: attend_slots(): jnp.concatenate([chosen[:, :, 0], suffix_kv[:, :, 0]], 1)]
    dot_general x8 -> x0, matrix products: 8.79 us -> none  [the longest x2 4.9 us: attend_slots(): jnp.einsum('sp,pltw->sltw', chooser, prompt_kv, preferred_element_type=jn...]
    select_n x5 -> x0, other arithmetic: 8.12 us -> none  [the longest x1 3.82 us: per_device(): jnp.where(lane_mask[:, None, None, None], packed[None], jnp.zeros((), jnp...]
    all_to_all x1 -> x0, starting transfers between devices: 7.28 us -> none  [per_device(): lax.all_to_all(outgoing, 'grp', split_axis=0, concat_axis=0, tiled=True)]
  transfers between devices with their start and end apart: 3 -> 0, of which waited for: 2 -> 0; matrix products, arithmetic and copies ran while one was open for 21% -> 0% of each run, Pallas kernels for 0% -> 0%
where the time goes in v1:
time: 33.8 us; the launch traced here: 33.4 us
  Pallas kernels  24.5 us (72%)
  local copies, waits for them, and re-layouts  8.21 us (24%)
  between operations  0.66 us (2%)
    pallas_call x1, Pallas kernels, per_device(): pl.pallas_call(functools.partial(kernel, groups, ranks), out_shape=jax.Sh...  24.5 us
    unnamed x18, local copies, waits for them, and re-layouts  7.6 us

profile of v1, /device:TPU:0, one launch (start us, length us, event | category | flops | bytes accessed | tf_op | source)
XLA Modules:
  0.0 33.4 jit_solution(7703700265694524707)
XLA Ops:
  0.6 0.0 copy-start
  0.6 1.6 %copy-done = bf16[4,512,2,256]{3,2,1,0:T(2,128)(2,1)S(1)} copy-done((bf16[4,512,2,256]{3,2,1,0:T(2,128)(2,1)S(1)}, bf16[4,512,2,256]{3,2,1,0:T(2,128)(2,1)}, u32[]{:S(2)}) %copy-start) | copy-done | bytes 2097176
  2.2 0.0 copy-start.1
  2.2 1.2 %copy-done.1 = bf16[2,512,2,256]{3,2,1,0:T(2,128)(2,1)S(1)} copy-done((bf16[2,512,2,256]{3,2,1,0:T(2,128)(2,1)S(1)}, bf16[2,512,2,256]{3,2,1,0:T(2,128)(2,1)}, u32[]{:S(2)}) %copy-start.1) | copy-done | bytes 1048600
  3.5 0.0 copy-start.2
  3.5 0.7 %copy-done.2 = bf16[4,2048]{1,0:T(4,128)(2,1)S(1)} copy-done((bf16[4,2048]{1,0:T(4,128)(2,1)S(1)}, bf16[4,2048]{1,0:T(4,128)(2,1)}, u32[]{:S(2)}) %copy-start.2) | copy-done | bytes 16408
  4.2 0.0 copy-start.3
  4.2 0.7 %copy-done.3 = bf16[4,2048]{1,0:T(4,128)(2,1)S(1)} copy-done((bf16[4,2048]{1,0:T(4,128)(2,1)S(1)}, bf16[4,2048]{1,0:T(4,128)(2,1)}, u32[]{:S(2)}) %copy-start.3) | copy-done | bytes 16408
  4.9 0.0 copy-start.4
  4.9 0.7 %copy-done.4 = bf16[4,2,256]{2,1,0:T(2,128)(2,1)S(1)} copy-done((bf16[4,2,256]{2,1,0:T(2,128)(2,1)S(1)}, bf16[4,2,256]{2,1,0:T(2,128)(2,1)}, u32[]{:S(2)}) %copy-start.4) | copy-done | bytes 4120
  5.6 0.0 copy-start.5
  5.6 0.7 %copy-done.5 = bf16[4,2,256]{2,1,0:T(2,128)(2,1)S(1)} copy-done((bf16[4,2,256]{2,1,0:T(2,128)(2,1)S(1)}, bf16[4,2,256]{2,1,0:T(2,128)(2,1)}, u32[]{:S(2)}) %copy-start.5) | copy-done | bytes 4120
  6.3 0.0 copy-start.6
  6.3 0.7 %copy-done.6 = s32[2,5]{1,0:T(2,128)S(1)} copy-done((s32[2,5]{1,0:T(2,128)S(1)}, s32[2,5]{1,0:T(2,128)}, u32[]{:S(2)}) %copy-start.6) | copy-done | bytes 64
  6.9 0.0 copy-start.7
  6.9 0.7 %copy-done.7 = s32[32]{0:T(128)S(1)} copy-done((s32[32]{0:T(128)S(1)}, s32[32]{0:T(128)}, u32[]{:S(2)}) %copy-start.7) | copy-done | bytes 152
  7.6 0.0 copy-start.8
  7.6 0.7 %copy-done.8 = s32[4]{0:T(128)S(1)} copy-done((s32[4]{0:T(128)S(1)}, s32[4]{0:T(128)}, u32[]{:S(2)}) %copy-start.8) | copy-done | bytes 40
  8.3 24.5 %shard_map.113 = bf16[8,1024]{1,0:T(8,128)(2,1)S(1)} custom-call(s32[32]{0:T(128)S(1)} %copy-done.7, s32[4]{0:T(128)S(1)} %copy-done.8, s32[2,5]{1,0:T(2,128)S(1)} %copy-done.6, bf16[4,512,2,256]{3,2,1,0:T(2,128)(2,1)S(1)} %copy-done, bf16[2,512,2,256]{3,2,1,0:T(2,128)(2,1)S(1)} %copy-done.1, bf16[4,2048]{1,0:T(4,128)(2,1)S(1)} %copy-done.2, ...), custom_call_target="tpu_custom_call" | custom-call | tf_op jit(solution)/shard_map/pallas_call | solution.py:323
  32.8 0.6 %fusion = (bf16[4,1024]{1,0:T(4,128)(2,1)}, bf16[4,1024]{1,0:T(4,128)(2,1)}) fusion(bf16[8,1024]{1,0:T(8,128)(2,1)S(1)} %shard_map.113), kind=kLoop, calls=%fused_computation | loop fusion | bytes 32768 | tf_op jit(solution)/shard_map/slice | solution.py:362
Async XLA Ops:
  0.6 1.6 %copy-start = (bf16[4,512,2,256]{3,2,1,0:T(2,128)(2,1)S(1)}, bf16[4,512,2,256]{3,2,1,0:T(2,128)(2,1)}, u32[]{:S(2)}) copy-start(bf16[4,512,2,256]{3,2,1,0:T(2,128)(2,1)} %suffix_hbm.1) | copy-start | bytes 6291460
  2.2 1.2 %copy-start.1 = (bf16[2,512,2,256]{3,2,1,0:T(2,128)(2,1)S(1)}, bf16[2,512,2,256]{3,2,1,0:T(2,128)(2,1)}, u32[]{:S(2)}) copy-start(bf16[2,512,2,256]{3,2,1,0:T(2,128)(2,1)} %prompt_hbm.1) | copy-start | bytes 3145732
  3.5 0.7 %copy-start.2 = (bf16[4,2048]{1,0:T(4,128)(2,1)S(1)}, bf16[4,2048]{1,0:T(4,128)(2,1)}, u32[]{:S(2)}) copy-start(bf16[4,2048]{1,0:T(4,128)(2,1)} %q1_ref.1) | copy-start | bytes 49156
  4.2 0.7 %copy-start.3 = (bf16[4,2048]{1,0:T(4,128)(2,1)S(1)}, bf16[4,2048]{1,0:T(4,128)(2,1)}, u32[]{:S(2)}) copy-start(bf16[4,2048]{1,0:T(4,128)(2,1)} %q2_ref.1) | copy-start | bytes 49156
  4.9 0.7 %copy-start.4 = (bf16[4,2,256]{2,1,0:T(2,128)(2,1)S(1)}, bf16[4,2,256]{2,1,0:T(2,128)(2,1)}, u32[]{:S(2)}) copy-start(bf16[4,2,256]{2,1,0:T(2,128)(2,1)} %f1_ref.1) | copy-start | bytes 12292
  5.6 0.7 %copy-start.5 = (bf16[4,2,256]{2,1,0:T(2,128)(2,1)S(1)}, bf16[4,2,256]{2,1,0:T(2,128)(2,1)}, u32[]{:S(2)}) copy-start(bf16[4,2,256]{2,1,0:T(2,128)(2,1)} %f2_ref.1) | copy-start | bytes 12292
  6.3 0.7 %copy-start.6 = (s32[2,5]{1,0:T(2,128)S(1)}, s32[2,5]{1,0:T(2,128)}, u32[]{:S(2)}) copy-start(s32[2,5]{1,0:T(2,128)} %moves_ref.1) | copy-start | bytes 124
  6.9 0.7 %copy-start.7 = (s32[32]{0:T(128)S(1)}, s32[32]{0:T(128)}, u32[]{:S(2)}) copy-start(s32[32]{0:T(128)} %lens_ref.1) | copy-start | bytes 388
  7.6 0.7 %copy-start.8 = (s32[4]{0:T(128)S(1)}, s32[4]{0:T(128)}, u32[]{:S(2)}) copy-start(s32[4]{0:T(128)} %pslot_ref.1) | copy-start | bytes 52

commit v2 on v1

v2 whole, which is shorter than its diff:
```python
import functools

import jax
import jax.numpy as jnp
from jax import lax
from jax.experimental import pallas as pl
from jax.experimental.pallas import tpu as pltpu
from jax.sharding import PartitionSpec as P

QH = 64
KVH = 8
HD = 128
MESH = pl.DeviceIdType.MESH
F32 = jnp.float32
BF16 = jnp.bfloat16


def kernel(
    groups,
    ranks,
    suffix_hbm,
    prompt_hbm,
    q1_hbm,
    f1_hbm,
    q2_hbm,
    f2_hbm,
    weight_hbm,
    lens_hbm,
    pslot_hbm,
    moves_hbm,
    out_ref,
    sbuf,
    pbuf,
    wbuf,
    q1_ref,
    f1_ref,
    q2_ref,
    f2_ref,
    lens_ref,
    pslot_ref,
    moves_ref,
    qs,
    fs,
    fresh_in,
    packets,
    parts_out,
    parts_in,
    rows_back,
    small_sem,
    kv_sem,
    w_sem,
    g_send,
    g_recv,
    r_send,
    r_recv,
    b_send,
    b_recv,
):
    me = lax.axis_index("grp")
    rank = lax.axis_index("tp")
    slots = q1_ref.shape[0]
    prompts = prompt_hbm.shape[0]
    features = q1_ref.shape[1]
    heads = features // HD
    share = QH // KVH
    kv_heads = heads // share
    width = kv_heads * HD
    cap = suffix_hbm.shape[1]
    plen = prompt_hbm.shape[1]
    cols = out_ref.shape[1]
    move_count = moves_ref.shape[0]

    barrier = pltpu.get_barrier_semaphore()
    for t in range(1, groups):
        pl.semaphore_signal(
            barrier, inc=1, device_id=(lax.rem(me + t, groups), rank), device_id_type=MESH
        )
    for t in range(1, ranks):
        pl.semaphore_signal(
            barrier, inc=1, device_id=(me, lax.rem(rank + t, ranks)), device_id_type=MESH
        )

    small = [
        pltpu.make_async_copy(src, dst, small_sem.at[i])
        for i, (src, dst) in enumerate(
            [
                (moves_hbm, moves_ref),
                (q2_hbm, q2_ref),
                (f2_hbm, f2_ref),
                (lens_hbm, lens_ref),
                (pslot_hbm, pslot_ref),
                (q1_hbm, q1_ref),
                (f1_hbm, f1_ref),
            ]
        )
    ]
    kv_copies = []
    for k in range(kv_heads):
        lanes = pl.ds(k * HD, HD)
        for p in range(prompts):
            kv_copies.append(
                pltpu.make_async_copy(
                    prompt_hbm.at[p, :, :, lanes], pbuf.at[p, k], kv_sem.at[p, k]
                )
            )
        for s in range(slots):
            kv_copies.append(
                pltpu.make_async_copy(
                    suffix_hbm.at[s, :, :, lanes], sbuf.at[s, k], kv_sem.at[prompts + s, k]
                )
            )

    def weight_copy(t):
        j = lax.rem(rank + t, ranks)
        return pltpu.make_async_copy(
            weight_hbm.at[:, pl.ds(pl.multiple_of(j * cols, cols), cols)], wbuf.at[t], w_sem.at[t]
        )

    steps = [t % ranks for t in range(1, ranks + 1)]
    for copy in small:
        copy.start()
    for copy in kv_copies:
        copy.start()
    for t in steps:
        weight_copy(t).start()
    for copy in small:
        copy.wait()

    zero = jnp.int32(0)
    out_slot, into_group, in_slot, from_group = zero - 1, zero, zero - 1, zero
    for m in range(move_count):
        leaves = moves_ref[m, 0] == me
        enters = moves_ref[m, 2] == me
        out_slot = jnp.where(leaves, moves_ref[m, 1], out_slot)
        into_group = jnp.where(leaves, moves_ref[m, 2], into_group)
        in_slot = jnp.where(enters, moves_ref[m, 3], in_slot)
        from_group = jnp.where(enters, moves_ref[m, 0], from_group)

    rows = 2 * slots
    qs[0:slots] = q1_ref[...].astype(F32)
    qs[slots:rows] = q2_ref[...].astype(F32)
    stacked = jnp.concatenate([qs[:, j * HD : (j + 1) * HD] for j in range(heads)], 0).astype(BF16)
    total = heads * rows

    pick = (
        lax.broadcasted_iota(jnp.int32, (heads, total), 1)
        == lax.broadcasted_iota(jnp.int32, (heads, total), 0) * rows + slots + in_slot
    ).astype(F32).astype(BF16)
    packets[me, 0:heads] = jnp.dot(pick, stacked, preferred_element_type=F32)
    fresh2 = [f2_ref[s].astype(F32) for s in range(slots)]
    own_fresh = jnp.zeros((2, width), F32)
    for s in range(slots):
        own_fresh = jnp.where(in_slot == s, fresh2[s], own_fresh)
    for k in range(kv_heads):
        packets[me, heads + 2 * k : heads + 2 * k + 2] = own_fresh[:, k * HD : (k + 1) * HD]

    pl.semaphore_wait(barrier, groups - 1 + ranks - 1)

    def gather_copy(t):
        return pltpu.make_async_remote_copy(
            src_ref=packets.at[me],
            dst_ref=packets.at[me],
            send_sem=g_send.at[t],
            recv_sem=g_recv.at[t],
            device_id=(lax.rem(me + t, groups), rank),
            device_id_type=MESH,
        )

    for t in range(1, groups):
        gather_copy(t).start()

    for s in range(slots):
        fs[s, 0:2] = f1_ref[s].astype(F32)
        fs[s, 2:4] = fresh2[s]
        fs[s, 4:8] = jnp.zeros((4, width), F32)

    mine = 2 * heads

    def source_of(r):
        s = r // mine
        k = (r % mine) // (2 * share)
        step = (r % (2 * share)) // share
        g = r % share
        return (k * share + g) * rows + step * slots + s

    swap = (
        source_of(lax.broadcasted_iota(jnp.int32, (total, total), 0))
        == lax.broadcasted_iota(jnp.int32, (total, total), 1)
    ).astype(F32).astype(BF16)
    back = (
        source_of(lax.broadcasted_iota(jnp.int32, (total, total), 1))
        == lax.broadcasted_iota(jnp.int32, (total, total), 0)
    ).astype(F32).astype(BF16)
    queries = jnp.dot(swap, stacked, preferred_element_type=F32)

    for copy in kv_copies:
        copy.wait()

    scale = HD ** (-0.5)
    low = -1e30
    nt = (((1,), (1,)), ((), ()))
    flat_p = pbuf.reshape(prompts, kv_heads, 2 * plen, HD)
    flat_s = sbuf.reshape(slots, kv_heads, 2 * cap, HD)
    p_col = lax.broadcasted_iota(jnp.int32, (1, 2 * plen), 1)
    s_col = lax.broadcasted_iota(jnp.int32, (1, 2 * cap), 1)
    f_col = lax.broadcasted_iota(jnp.int32, (1, 8), 1)
    p_valid = (p_col % 2) == 0
    s_even = (s_col % 2) == 0

    def attend(q, head_of, second, s, fval):
        wide = jnp.concatenate(
            [jnp.where(head_of == k, q, 0.0) for k in range(kv_heads)], 1
        ).astype(BF16)
        row = jnp.maximum(pslot_ref[s], 0)
        n = lens_ref[me * slots + s]
        xp = jnp.concatenate([flat_p[row, k] for k in range(kv_heads)], 1)
        xs = jnp.concatenate([flat_s[s, k] for k in range(kv_heads)], 1)
        xf = fval.astype(BF16)
        sp = lax.dot_general(wide, xp, nt, preferred_element_type=F32) * scale
        ss = lax.dot_general(wide, xs, nt, preferred_element_type=F32) * scale
        sf = lax.dot_general(wide, xf, nt, preferred_element_type=F32) * scale
        sp = jnp.where(p_valid, sp, low)
        ss = jnp.where(s_even & (s_col < 2 * n), ss, low)
        sf = jnp.where((f_col == 0) | ((f_col == 2) & second), sf, low)
        top = jnp.maximum(
            jnp.maximum(jnp.max(sp, 1, keepdims=True), jnp.max(ss, 1, keepdims=True)),
            jnp.max(sf, 1, keepdims=True),
        )
        ep, es, ef = jnp.exp(sp - top), jnp.exp(ss - top), jnp.exp(sf - top)
        inv = 1.0 / (
            jnp.sum(ep, 1, keepdims=True)
            + jnp.sum(es, 1, keepdims=True)
            + jnp.sum(ef, 1, keepdims=True)
        )

        def shifted(e):
            w = e * inv
            return jnp.concatenate(
                [pltpu.roll(w[:, i : i + HD], 1, 1) for i in range(0, e.shape[1], HD)], 1
            ).astype(BF16)

        mixed = jnp.dot(shifted(ep), xp, preferred_element_type=F32)
        mixed += jnp.dot(shifted(es), xs, preferred_element_type=F32)
        wf = (ef * inv).astype(BF16).astype(F32)
        mixed += wf[:, 0:1] * fval[1:2] + wf[:, 2:3] * fval[3:4]
        picked = mixed[:, :HD]
        for k in range(1, kv_heads):
            picked = jnp.where(head_of == k, mixed[:, k * HD : (k + 1) * HD], picked)
        return jnp.where(pslot_ref[s] >= 0, picked, 0.0)

    q_row = lax.broadcasted_iota(jnp.int32, (mine, 1), 0)
    results = [
        attend(
            queries[s * mine : (s + 1) * mine],
            q_row // (2 * share),
            (q_row % (2 * share)) >= share,
            s,
            fs[s],
        )
        for s in range(slots)
    ]
    attn = jnp.concatenate(results, 0).astype(BF16)
    attn = jnp.dot(back, attn, preferred_element_type=F32)

    for t in range(1, groups):
        gather_copy(t).wait()
    leaver = jnp.maximum(out_slot, 0)
    foreign = packets[into_group]
    fresh_in[...] = jnp.zeros((8, width), F32)
    for k in range(kv_heads):
        fresh_in[2:4, k * HD : (k + 1) * HD] = foreign[heads + 2 * k : heads + 2 * k + 2]
    fresh_in[0:2] = f1_ref[leaver].astype(F32)
    h_row = lax.broadcasted_iota(jnp.int32, (heads, 1), 0)
    guest = attend(foreign[:heads], h_row // share, h_row >= 0, leaver, fresh_in[...])
    r_row = lax.broadcasted_iota(jnp.int32, (rows, 1), 0)
    going = (r_row == slots + out_slot) & (out_slot >= 0)
    attn = jnp.concatenate(
        [
            jnp.where(going, guest[j : j + 1], attn[j * rows : (j + 1) * rows])
            for j in range(heads)
        ],
        1,
    ).astype(BF16)

    def part_copy(t):
        return pltpu.make_async_remote_copy(
            src_ref=parts_out.at[t],
            dst_ref=parts_in.at[t],
            send_sem=r_send.at[t],
            recv_sem=r_recv.at[t],
            device_id=(me, lax.rem(rank + t, ranks)),
            device_id_type=MESH,
        )

    result = None
    for t in steps:
        weight_copy(t).wait()
        part = jnp.dot(attn, wbuf[t], preferred_element_type=F32)
        if t:
            parts_out[t] = part.astype(BF16)
            part_copy(t).start()
        else:
            result = part
    for t in range(1, ranks):
        part_copy(t).wait()
        result += parts_in[t].astype(F32)

    rows_back[me] = jnp.sum(jnp.where(going, result, 0.0), 0, keepdims=True)

    def back_copy(t):
        return pltpu.make_async_remote_copy(
            src_ref=rows_back.at[me],
            dst_ref=rows_back.at[me],
            send_sem=b_send.at[t],
            recv_sem=b_recv.at[t],
            device_id=(lax.rem(me + t, groups), rank),
            device_id_type=MESH,
        )

    for t in range(1, groups):
        back_copy(t).start()
    for t in range(1, groups):
        back_copy(t).wait()
    coming = (r_row == slots + in_slot) & (in_slot >= 0)
    result = jnp.where(coming, rows_back[from_group], jnp.where(going, 0.0, result))
    out_ref[...] = result.astype(BF16)


def per_device(
    suffix_cache,
    prompt_cache,
    query_first,
    fresh_first,
    query_second,
    fresh_second,
    out_weight,
    suffix_len,
    prompt_slot,
    moves,
):
    groups, ranks = lax.axis_size("grp"), lax.axis_size("tp")
    slots, features = query_first.shape
    prompts, plen = prompt_cache.shape[:2]
    cap = suffix_cache.shape[1]
    width = suffix_cache.shape[3]
    kv_heads = width // HD
    heads = features // HD
    cols = out_weight.shape[1] // ranks
    depth = out_weight.shape[0]
    vmem = pl.BlockSpec(memory_space=pltpu.VMEM)
    hbm = pl.BlockSpec(memory_space=pltpu.HBM)
    dma = pltpu.SemaphoreType.DMA
    out = pl.pallas_call(
        functools.partial(kernel, groups, ranks),
        out_shape=jax.ShapeDtypeStruct((2 * slots, cols), BF16),
        in_specs=[hbm] * 10,
        out_specs=vmem,
        scratch_shapes=[
            pltpu.VMEM((slots, kv_heads, cap, 2, HD), BF16),
            pltpu.VMEM((prompts, kv_heads, plen, 2, HD), BF16),
            pltpu.VMEM((ranks, depth, cols), BF16),
            pltpu.VMEM((slots, features), BF16),
            pltpu.VMEM((slots, 2, width), BF16),
            pltpu.VMEM((slots, features), BF16),
            pltpu.VMEM((slots, 2, width), BF16),
            pltpu.SMEM(suffix_len.shape, jnp.int32),
            pltpu.SMEM(prompt_slot.shape, jnp.int32),
            pltpu.SMEM(moves.shape, jnp.int32),
            pltpu.VMEM((2 * slots, features), F32),
            pltpu.VMEM((slots, 8, width), F32),
            pltpu.VMEM((8, width), F32),
            pltpu.VMEM((groups, heads + 8, HD), F32),
            pltpu.VMEM((ranks, 2 * slots, cols), BF16),
            pltpu.VMEM((ranks, 2 * slots, cols), BF16),
            pltpu.VMEM((groups, 1, cols), F32),
            dma((7,)),
            dma((prompts + slots, kv_heads)),
            dma((ranks,)),
            dma((groups,)),
            dma((groups,)),
            dma((ranks,)),
            dma((ranks,)),
            dma((groups,)),
            dma((groups,)),
        ],
        compiler_params=pltpu.CompilerParams(
            collective_id=0, has_side_effects=True, vmem_limit_bytes=67043328
        ),
    )(
        suffix_cache,
        prompt_cache,
        query_first,
        fresh_first,
        query_second,
        fresh_second,
        out_weight,
        suffix_len,
        prompt_slot,
        moves,
    )
    return out[:slots], out[slots:]


def solution(mesh):
    placed = (
        P("grp", None, None, "tp"),
        P("grp", None, None, "tp"),
        P("grp", "tp"),
        P("grp", None, "tp"),
        P("grp", "tp"),
        P("grp", None, "tp"),
        P("tp", None),
        P(),
        P("grp"),
        P(),
    )
    return jax.shard_map(
        per_device,
        mesh=mesh,
        in_specs=placed,
        out_specs=(P("grp", "tp"), P("grp", "tp")),
        check_vma=False,
    )
```

time: 33.8 us -> 26.6 us (0.79)
  local copies, waits for them, and re-layouts: 8.21 us -> 1.4 us
    unnamed x18 -> x0, local copies, waits for them, and re-layouts: 7.6 us -> none
    slice x1, local copies, waits for them, and re-layouts: 0.61 us -> 1.4 us  [per_device(): return (out[:slots], out[slots:])]
where the time goes in v2:
time: 26.6 us; the launch traced here: 26.4 us
  Pallas kernels  24.4 us (92%)
  local copies, waits for them, and re-layouts  1.4 us (5%)
  between operations  0.64 us (2%)
    pallas_call x1, Pallas kernels, per_device(): pl.pallas_call(functools.partial(kernel, groups, ranks), out_shape=jax.Sh...  24.4 us
    slice x1, local copies, waits for them, and re-layouts, per_device(): return (out[:slots], out[slots:])  1.4 us

profile of v2, /device:TPU:0, one launch (start us, length us, event | category | flops | bytes accessed | tf_op | source)
XLA Modules:
  0.0 26.4 jit_solution(10004903189784265744)
XLA Ops:
  0.6 24.4 %shard_map.113 = bf16[8,1024]{1,0:T(8,128)(2,1)} custom-call(bf16[4,512,2,256]{3,2,1,0:T(2,128)(2,1)} %suffix_hbm.1, bf16[2,512,2,256]{3,2,1,0:T(2,128)(2,1)} %prompt_hbm.1, bf16[4,2048]{1,0:T(4,128)(2,1)} %q1_hbm.1, bf16[4,2,256]{2,1,0:T(2,128)(2,1)} %f1_hbm.1, bf16[4,2048]{1,0:T(4,128)(2,1)} %q2_hbm.1, bf16[4,2,256]{2,1,0:T(2,128)(2,1)} %f2_hbm.1, ...), custom_call_target="tpu_custom_call" | custom-call | tf_op jit(solution)/shard_map/pallas_call | solution.py:353
  25.0 1.4 %fusion = (bf16[4,1024]{1,0:T(4,128)(2,1)}, bf16[4,1024]{1,0:T(4,128)(2,1)}) fusion(bf16[8,1024]{1,0:T(8,128)(2,1)} %shard_map.113), kind=kLoop, calls=%fused_computation | loop fusion | bytes 32768 | tf_op jit(solution)/shard_map/slice | solution.py:401

commit v3 on v2

--- a/solution.py
+++ b/solution.py
@@ -42,10 +42,12 @@
     qs,
     fs,
     fresh_in,
+    pack,
     packets,
     parts_out,
     parts_in,
-    rows_back,
+    guest_out,
+    guest_in,
     small_sem,
     kv_sem,
     w_sem,
@@ -70,15 +72,22 @@
     cols = out_ref.shape[1]
     move_count = moves_ref.shape[0]
 
+    cores = 2 if ranks % 2 == 0 else 1
+
+    def rank_at(t):
+        chip = lax.rem(rank // cores + t // cores, ranks // cores)
+        return chip * cores + lax.rem(rank % cores + t % cores, cores)
+
     barrier = pltpu.get_barrier_semaphore()
-    for t in range(1, groups):
-        pl.semaphore_signal(
-            barrier, inc=1, device_id=(lax.rem(me + t, groups), rank), device_id_type=MESH
-        )
-    for t in range(1, ranks):
-        pl.semaphore_signal(
-            barrier, inc=1, device_id=(me, lax.rem(rank + t, ranks)), device_id_type=MESH
-        )
+    for u in range(groups):
+        for t in range(ranks):
+            if u or t:
+                pl.semaphore_signal(
+                    barrier,
+                    inc=1,
+                    device_id=(lax.rem(me + u, groups), rank_at(t)),
+                    device_id_type=MESH,
+                )
 
     small = [
         pltpu.make_async_copy(src, dst, small_sem.at[i])
@@ -111,12 +120,12 @@
             )
 
     def weight_copy(t):
-        j = lax.rem(rank + t, ranks)
+        j = rank_at(t)
         return pltpu.make_async_copy(
             weight_hbm.at[:, pl.ds(pl.multiple_of(j * cols, cols), cols)], wbuf.at[t], w_sem.at[t]
         )
 
-    steps = [t % ranks for t in range(1, ranks + 1)]
+    steps = list(range(cores, ranks)) + list(range(1, cores)) + [0]
     for copy in small:
         copy.start()
     for copy in kv_copies:
@@ -146,15 +155,17 @@
         lax.broadcasted_iota(jnp.int32, (heads, total), 1)
         == lax.broadcasted_iota(jnp.int32, (heads, total), 0) * rows + slots + in_slot
     ).astype(F32).astype(BF16)
-    packets[me, 0:heads] = jnp.dot(pick, stacked, preferred_element_type=F32)
+    pack[0:heads] = jnp.dot(pick, stacked, preferred_element_type=F32)
+    pack[heads:] = jnp.zeros((8, HD), F32)
     fresh2 = [f2_ref[s].astype(F32) for s in range(slots)]
     own_fresh = jnp.zeros((2, width), F32)
     for s in range(slots):
         own_fresh = jnp.where(in_slot == s, fresh2[s], own_fresh)
     for k in range(kv_heads):
-        packets[me, heads + 2 * k : heads + 2 * k + 2] = own_fresh[:, k * HD : (k + 1) * HD]
-
-    pl.semaphore_wait(barrier, groups - 1 + ranks - 1)
+        pack[heads + 2 * k : heads + 2 * k + 2] = own_fresh[:, k * HD : (k + 1) * HD]
+    packets[me] = pack[...].astype(BF16)
+
+    pl.semaphore_wait(barrier, groups * ranks - 1)
 
     def gather_copy(t):
         return pltpu.make_async_remote_copy(
@@ -265,7 +276,7 @@
     for t in range(1, groups):
         gather_copy(t).wait()
     leaver = jnp.maximum(out_slot, 0)
-    foreign = packets[into_group]
+    foreign = packets[into_group].astype(F32)
     fresh_in[...] = jnp.zeros((8, width), F32)
     for k in range(kv_heads):
         fresh_in[2:4, k * HD : (k + 1) * HD] = foreign[heads + 2 * k : heads + 2 * k + 2]
@@ -288,41 +299,46 @@
             dst_ref=parts_in.at[t],
             send_sem=r_send.at[t],
             recv_sem=r_recv.at[t],
-            device_id=(me, lax.rem(rank + t, ranks)),
+            device_id=(me, rank_at(t)),
             device_id_type=MESH,
         )
 
+    def guest_copy(u, t):
+        return pltpu.make_async_remote_copy(
+            src_ref=guest_out.at[t],
+            dst_ref=guest_in.at[me, t],
+            send_sem=b_send.at[u, t],
+            recv_sem=b_recv.at[u, t],
+            device_id=(lax.rem(me + u, groups), rank_at(t)),
+            device_id_type=MESH,
+        )
+
+    guest_in[me] = jnp.zeros(guest_in.shape[1:], BF16)
     result = None
     for t in steps:
         weight_copy(t).wait()
         part = jnp.dot(attn, wbuf[t], preferred_element_type=F32)
+        alone = jnp.sum(jnp.where(going, part, 0.0), 0, keepdims=True)
+        guest_out[t] = jnp.concatenate(
+            [alone[:, i : i + HD] for i in range(0, cols, HD)], 0
+        ).astype(BF16)
         if t:
             parts_out[t] = part.astype(BF16)
             part_copy(t).start()
         else:
             result = part
+        for u in range(1, groups):
+            guest_copy(u, t).start()
     for t in range(1, ranks):
         part_copy(t).wait()
         result += parts_in[t].astype(F32)
-
-    rows_back[me] = jnp.sum(jnp.where(going, result, 0.0), 0, keepdims=True)
-
-    def back_copy(t):
-        return pltpu.make_async_remote_copy(
-            src_ref=rows_back.at[me],
-            dst_ref=rows_back.at[me],
-            send_sem=b_send.at[t],
-            recv_sem=b_recv.at[t],
-            device_id=(lax.rem(me + t, groups), rank),
-            device_id_type=MESH,
-        )
-
-    for t in range(1, groups):
-        back_copy(t).start()
-    for t in range(1, groups):
-        back_copy(t).wait()
+    for t in steps:
+        for u in range(1, groups):
+            guest_copy(u, t).wait()
+    arrived = jnp.sum(guest_in[from_group].astype(F32), 0)
+    arrived = jnp.concatenate([arrived[i : i + 1] for i in range(cols // HD)], 1)
     coming = (r_row == slots + in_slot) & (in_slot >= 0)
-    result = jnp.where(coming, rows_back[from_group], jnp.where(going, 0.0, result))
+    result = jnp.where(coming, arrived, jnp.where(going, 0.0, result))
     out_ref[...] = result.astype(BF16)
 
 
@@ -352,7 +368,7 @@
     dma = pltpu.SemaphoreType.DMA
     out = pl.pallas_call(
         functools.partial(kernel, groups, ranks),
-        out_shape=jax.ShapeDtypeStruct((2 * slots, cols), BF16),
+        out_shape=pltpu.VMEM((2 * slots, cols), BF16),
         in_specs=[hbm] * 10,
         out_specs=vmem,
         scratch_shapes=[
@@ -369,10 +385,12 @@
             pltpu.VMEM((2 * slots, features), F32),
             pltpu.VMEM((slots, 8, width), F32),
             pltpu.VMEM((8, width), F32),
-            pltpu.VMEM((groups, heads + 8, HD), F32),
+            pltpu.VMEM((heads + 8, HD), F32),
+            pltpu.VMEM((groups, heads + 8, HD), BF16),
             pltpu.VMEM((ranks, 2 * slots, cols), BF16),
             pltpu.VMEM((ranks, 2 * slots, cols), BF16),
-            pltpu.VMEM((groups, 1, cols), F32),
+            pltpu.VMEM((ranks, cols // HD, HD), BF16),
+            pltpu.VMEM((groups, ranks, cols // HD, HD), BF16),
             dma((7,)),
             dma((prompts + slots, kv_heads)),
             dma((ranks,)),
@@ -380,23 +398,28 @@
             dma((groups,)),
             dma((ranks,)),
             dma((ranks,)),
-            dma((groups,)),
-            dma((groups,)),
+            dma((groups, ranks)),
+            dma((groups, ranks)),
         ],
         compiler_params=pltpu.CompilerParams(
-            collective_id=0, has_side_effects=True, vmem_limit_bytes=67043328
+            collective_id=0, has_side_effects=True, vmem_limit_bytes=48 * 1024 * 1024
         ),
     )(
-        suffix_cache,
-        prompt_cache,
-        query_first,
-        fresh_first,
-        query_second,
-        fresh_second,
-        out_weight,
-        suffix_len,
-        prompt_slot,
-        moves,
+        *[
+            pltpu.with_memory_space_constraint(x, pltpu.HBM)
+            for x in (
+                suffix_cache,
+                prompt_cache,
+                query_first,
+                fresh_first,
+                query_second,
+                fresh_second,
+                out_weight,
+                suffix_len,
+                prompt_slot,
+                moves,
+            )
+        ]
     )
     return out[:slots], out[slots:]
 

time: 26.6 us -> 23.9 us (0.90)
  Pallas kernels: 24.4 us -> 22.5 us
  local copies, waits for them, and re-layouts: 1.4 us -> 0.61 us
    pallas_call x1, Pallas kernels: 24.4 us -> 22.5 us  [per_device(): pl.pallas_call(functools.partial(kernel, groups, ranks), out_shape=pltpu....]
    slice x1, local copies, waits for them, and re-layouts: 1.4 us -> 0.61 us  [per_device(): return (out[:slots], out[slots:])]
where the time goes in v3:
time: 23.9 us; the launch traced here: 23.8 us
  Pallas kernels  22.5 us (94%)
  between operations  0.64 us (3%)
  local copies, waits for them, and re-layouts  0.61 us (3%)
    pallas_call x1, Pallas kernels, per_device(): pl.pallas_call(functools.partial(kernel, groups, ranks), out_shape=pltpu....  22.5 us
    slice x1, local copies, waits for them, and re-layouts, per_device(): return (out[:slots], out[slots:])  0.61 us

profile of v3, /device:TPU:0, one launch (start us, length us, event | category | flops | bytes accessed | tf_op | source)
XLA Modules:
  0.0 23.8 jit_solution(15009717539251486550)
XLA Ops:
  0.6 22.5 %shard_map.113 = bf16[8,1024]{1,0:T(8,128)(2,1)S(1)} custom-call(bf16[4,512,2,256]{3,2,1,0:T(2,128)(2,1)} %suffix_hbm.1, bf16[2,512,2,256]{3,2,1,0:T(2,128)(2,1)} %prompt_hbm.1, bf16[4,2048]{1,0:T(4,128)(2,1)} %q1_hbm.1, bf16[4,2,256]{2,1,0:T(2,128)(2,1)} %f1_hbm.1, bf16[4,2048]{1,0:T(4,128)(2,1)} %q2_hbm.1, bf16[4,2,256]{2,1,0:T(2,128)(2,1)} %f2_hbm.1, ...), custom_call_target="tpu_custom_call" | custom-call | tf_op jit(solution)/shard_map/pallas_call | solution.py:369
  23.2 0.6 %fusion = (bf16[4,1024]{1,0:T(4,128)(2,1)}, bf16[4,1024]{1,0:T(4,128)(2,1)}) fusion(bf16[8,1024]{1,0:T(8,128)(2,1)S(1)} %shard_map.113), kind=kLoop, calls=%fused_computation | loop fusion | bytes 32768 | tf_op jit(solution)/shard_map/slice | solution.py:424
